TPU v7x, 32 devices: a whole 2x2x4 slice. The times are simulated.
32 devices in a mesh: ctx: 4 (over x, core), tp: 8 (over z, y).
Axes of the slice: x: 2, y: 2, z: 4, core: 2. Of those that a mesh axis runs over, the one named last changes fastest.
Arguments:
- token_ids: int32 [1024], replicated, may hold values from 0 to 128255
- doc_lengths: int32 [8], replicated, may hold values from 1 to 256, 1024 in all
- block_order: int32 [8], replicated, may hold values from 0 to 7, each once
- table: bfloat16 [128256, 8192], P('tp', 'ctx'), may hold values from -6 to 6
- gain: float32 [8192], replicated, may hold values from 0.5 to 12, as said below
- w_query: bfloat16 [8192, 8192], P('ctx', 'tp'), may hold values from -0.0625 to 0.0625
- w_keyval: bfloat16 [8192, 2, 1024], P('ctx'), may hold values from -0.0625 to 0.0625
Outputs:
- attended: bfloat16 [1024, 8192], P('ctx', 'tp')
Inputs may be any that keep to these rules, and one draw needn't show every extreme that they name: `token_ids`: ids of the vocabulary. `doc_lengths`: the documents fill the slab in order, their lengths sum to 1024. `block_order`: a permutation of the 8 blocks of the slab. `gain`: positive gains.
All inputs are finite; a program needn't handle non-finite values.
Results may differ from a plain program's by a relative error of at most 0.007.
The roundings to bfloat16 on the way count: a program that leaves them out, or rounds other values in their place, can miss the bound.
Values may be sent and summed in bfloat16 or wider, within the bound.
A program may use at most 128 MiB of HBM per device.

v0:
```python
import jax
import jax.numpy as jnp
from jax import lax
from jax.sharding import PartitionSpec as P

HEADS = 64
KV_HEADS = 8
HD = 128
BLOCK = 128
rotary_base = 500000.0


def rotary(values_in, pos_rows):
    half_dim = values_in.shape[-1] // 2
    steps_up = jnp.arange(half_dim, dtype=jnp.float32)
    freqs = jnp.power(rotary_base, -2.0 * steps_up / values_in.shape[-1])
    angle = pos_rows.astype(jnp.float32)[:, None] * freqs[None, :]
    angle = angle.reshape((angle.shape[0],) + (1,) * (values_in.ndim - 2) + (half_dim,))
    cosine = jnp.cos(angle)
    sine = jnp.sin(angle)
    first = values_in[..., :half_dim]
    second = values_in[..., half_dim:]
    return jnp.concatenate(
        [first * cosine - second * sine, second * cosine + first * sine], axis=-1
    )


def document_of(pos_rows, doc_lengths):
    ends = jnp.cumsum(doc_lengths)
    return jnp.sum((ends[None, :] <= pos_rows[:, None]).astype(jnp.int32), axis=1)


def shards(token_ids, doc_lengths, block_order, table, gain, w_query, w_keyval):
    ctx_count = lax.axis_size("ctx")
    ctx_at = lax.axis_index("ctx")
    tp_count = lax.axis_size("tp")
    tp_at = lax.axis_index("tp")
    tokens_all = token_ids.shape[0]
    tok_here = tokens_all // ctx_count
    vocab_here = table.shape[0]
    columns = table.shape[1]
    width = gain.shape[0]
    heads_here = HEADS // tp_count
    row_index = jnp.arange(tokens_all, dtype=jnp.int32)
    positions = block_order[row_index // BLOCK] * BLOCK + row_index % BLOCK
    local_ids = token_ids[positions] - tp_at * vocab_here
    inside = (local_ids >= 0) & (local_ids < vocab_here)
    picked = jnp.take(table, jnp.clip(local_ids, 0, vocab_here - 1), axis=0)
    partial_value = jnp.where(inside[:, None], picked, jnp.zeros_like(picked))
    kv_head = tp_at * heads_here // (HEADS // KV_HEADS)
    w_pair = lax.dynamic_slice_in_dim(w_keyval, kv_head * HD, HD, 2).reshape(
        w_keyval.shape[0], 2 * HD
    )
    col_embed = lax.psum(partial_value, "tp").astype(jnp.float32)
    gain_here = lax.dynamic_slice_in_dim(gain, ctx_at * columns, columns)
    col_scaled = (col_embed * gain_here).astype(jnp.bfloat16)
    query_term = jnp.dot(col_scaled, w_query, preferred_element_type=jnp.float32)
    pair_term = jnp.dot(col_scaled, w_pair, preferred_element_type=jnp.float32)
    square_term = jnp.sum(col_embed * col_embed, axis=1)
    query_raw, pair_raw, sumsq = (
        lax.psum_scatter(query_term, "ctx", scatter_dimension=0, tiled=True),
        lax.psum_scatter(pair_term, "ctx", scatter_dimension=0, tiled=True),
        lax.psum_scatter(square_term, "ctx", scatter_dimension=0, tiled=True),
    )
    inverse = lax.rsqrt(sumsq / width + 1e-05)
    my_pos = lax.dynamic_slice_in_dim(positions, ctx_at * tok_here, tok_here)
    query_rows = rotary(
        (query_raw * inverse[:, None]).reshape(tok_here, heads_here, HD), my_pos
    ).astype(jnp.bfloat16)
    key_rows = rotary(pair_raw[:, :HD] * inverse[:, None], my_pos).astype(jnp.bfloat16)
    value_rows = (pair_raw[:, HD:] * inverse[:, None]).astype(jnp.bfloat16)
    my_doc = document_of(my_pos, doc_lengths)
    stacked = jnp.transpose(query_rows, (1, 0, 2)).reshape(heads_here * tok_here, HD)
    query_pos = jnp.tile(my_pos, heads_here)
    query_doc = jnp.tile(my_doc, heads_here)
    inv_root = 1.0 / jnp.sqrt(jnp.float32(HD))
    query_total = heads_here * tok_here
    key_piece = lax.all_gather(key_rows, "ctx", axis=0, tiled=True)
    value_piece = lax.all_gather(value_rows, "ctx", axis=0, tiled=True)
    key_doc = document_of(positions, doc_lengths)
    allowed = (key_doc[None, :] == query_doc[:, None]) & (positions[None, :] <= query_pos[:, None])
    largest = jnp.full((query_total,), -1e30, jnp.float32)
    scores = (
        lax.dot_general(
            stacked, key_piece, (((1,), (1,)), ((), ())), preferred_element_type=jnp.float32
        )
        * inv_root
    )
    masked = jnp.where(allowed, scores, jnp.float32(-1e30))
    new_largest = jnp.maximum(largest, jnp.max(masked, axis=1))
    weights = jnp.where(allowed, jnp.exp(masked - new_largest[:, None]), jnp.float32(0.0))
    new_totals = jnp.sum(weights, axis=1)
    new_accum = jnp.dot(
        weights.astype(jnp.bfloat16), value_piece, preferred_element_type=jnp.float32
    )
    mixed = (new_accum / new_totals[:, None]).reshape(heads_here, tok_here, HD)
    return jnp.transpose(mixed, (1, 0, 2)).reshape(tok_here, heads_here * HD).astype(jnp.bfloat16)


def solution(mesh):
    in_specs = (P(), P(), P(), P("tp", "ctx"), P(), P("ctx", "tp"), P("ctx", None, None))
    out_specs = P("ctx", "tp")
    return jax.shard_map(shards, mesh=mesh, in_specs=in_specs, out_specs=out_specs, check_vma=False)
```

profile of v0, /device:TPU:0, one launch (start us, length us, event | category | flops | bytes accessed | tf_op | source)
XLA Modules:
  0.0 328.4 jit_solution(2111878941764237552)
XLA Ops:
  6.6 1.6 fusion.32
  8.2 4.3 %compare_select_fusion.3 = s32[1024,1]{0,1:T(1,128)S(1)} fusion(s32[]{:T(128)} %bitcast.3, s32[]{:T(128)} %bitcast.4, s32[]{:T(128)} %bitcast.5, s32[]{:T(128)} %bitcast.6, s32[]{:T(128)} %bitcast.7, s32[]{:T(128)} %bitcast.9, s32[]{:T(128)} %bitcast.8), kind=kLoop, calls=%fused_computation.38 | loop fusion | flops 23552 | bytes 4124 | tf_op jit(solution)/shard_map/gather | solution.py:45
  12.5 0.7 fusion.21
  13.2 4.5 %gather_fusion = s32[1024]{0:T(1024)S(1)} fusion(s32[1024]{0:T(1024)S(1)} %copy-done, s32[1024]{0:T(1024)S(1)} %broadcast_clamp_fusion.1), kind=kCustom, calls=%fused_computation | custom fusion | bytes 12288 | tf_op jit(solution)/shard_map/gather | solution.py:46
  17.8 52.7 %gather_fusion.1 = bf16[1024,2048]{1,0:T(8,128)(2,1)} fusion(bf16[16032,2048]{1,0:T(8,128)(2,1)} %param.10, s32[1024]{0:T(1024)S(1)} %broadcast_clamp_fusion), kind=kCustom, calls=%fused_computation.1 | custom fusion | bytes 8392704 | tf_op jit(solution)/shard_map/jit(_take)/gather | solution.py:48
  70.5 4.1 %select_select_fusion = bf16[1024,2048]{1,0:T(8,128)(2,1)} fusion(bf16[1024,2048]{1,0:T(8,128)(2,1)} %gather_fusion.1, pred[1024]{0:T(1024)(128)(4,1)S(1)} %get-tuple-element.9, pred[1024]{0:T(1024)(128)(4,1)S(1)} %get-tuple-element.19), kind=kLoop, calls=%fused_computation.12 | loop fusion | flops 4194304 | bytes 8390656 | tf_op jit(solution)/shard_map/jit(_where)/select_n | solution.py:49
  74.7 0.7 dynamic_slice.10
  75.4 1.8 constant_dynamic-slice_fusion
  77.2 156.5 %all-reduce.3.cloned.1.call-done = bf16[1024,2048]{1,0:T(8,128)(2,1)} async-done(((bf16[1024,2048]{1,0:T(8,128)(2,1)}), bf16[1024,2048]{1,0:T(8,128)(2,1)}) %all-reduce.3.cloned.1.call-update) | async-done | bytes 4194320 | tf_op jit(solution)/shard_map/psum | solution.py:54
  233.7 4.4 %fusion.7 = f32[1024,256]{1,0:T(8,128)} fusion(bf16[1024,2048]{1,0:T(8,128)(2,1)} %all-reduce.3.cloned.1.call-done, f32[2048]{0:T(1024)S(1)} %dynamic_slice.10, bf16[256,8,2,128]{3,2,1,0:T(2,128)(2,1)S(1)} %bitcast.44), kind=kOutput, calls=%fused_computation.14 | convolution fusion | flops 1080033280 | bytes 6299648 | tf_op jit(solution)/shard_map/dot_general | solution.py:58
  238.2 9.9 %fusion.9 = f32[1024,1024]{1,0:T(8,128)} fusion(bf16[2048,1024]{1,0:T(8,128)(2,1)} %param.12, bf16[1024,2048]{1,0:T(8,128)(2,1)} %all-reduce.3.cloned.1.call-done, f32[2048]{0:T(1024)S(1)} %dynamic_slice.10), kind=kOutput, calls=%fused_computation.15 | convolution fusion | flops 4301258752 | bytes 12591104 | tf_op jit(solution)/shard_map/dot_general | solution.py:57
  248.2 0.2 reduce-window.8
  248.4 0.1 convert_reduce_fusion.1
  248.5 0.6 dynamic-slice
  249.9 3.1 fusion.1
  253.0 7.3 %all-reduce = f32[1024]{0:T(1024)S(1)} all-reduce(f32[1024]{0:T(1024)S(1)} %fusion.1), channel_id=3, replica_groups=mesh['ctx'=4,'tp'=8] {'ctx'}, use_global_device_ids=true, to_apply=%region_6.7.clone | all-reduce | flops 1024 | bytes 8192
  260.3 1.9 reduce-scatter.5.cloned.1.call-done
  262.2 1.1 slice_multiply_fusion.1
  263.2 0.6 subtract_convert_fusion.1
  263.8 0.1 pad_maximum_fusion.1
  263.9 5.8 %all_gather.6 = bf16[1024,128]{1,0:T(8,128)(2,1)S(1)} all-gather(bf16[256,128]{1,0:T(8,128)(2,1)S(1)} %pad_maximum_fusion.1), channel_id=1, replica_groups=mesh['ctx'=4,'tp'=8] {'ctx'}, dimensions={0}, use_global_device_ids=true | all-gather | bytes 327680 | tf_op jit(solution)/shard_map/all_gather | solution.py:78
  269.7 6.0 %all_gather.7 = bf16[1024,128]{1,0:T(8,128)(2,1)S(1)} all-gather(bf16[256,128]{1,0:T(8,128)(2,1)S(1)} %get-tuple-element.16), channel_id=1, replica_groups=mesh['ctx'=4,'tp'=8] {'ctx'}, dimensions={0}, use_global_device_ids=true | all-gather | bytes 327680 | tf_op jit(solution)/shard_map/all_gather | solution.py:79
  275.7 33.6 %reduce-scatter.3.cloned.1.call-done = f32[256,1024]{1,0:T(8,128)} async-done(((f32[1024,1024]{1,0:T(8,128)}), f32[256,1024]{1,0:T(8,128)}) %reduce-scatter.3.cloned.1.call-update) | async-done | bytes 1048592 | tf_op jit(solution)/shard_map/reduce_scatter | solution.py:61
  309.3 1.4 multiply_bitcast_fusion
  310.7 0.2 copy.23
  310.9 0.3 fusion.31
  311.2 0.4 subtract_convert_fusion
  311.6 0.3 pad_maximum_fusion
  311.9 2.1 fusion.2
  314.1 3.8 %fusion.3 = f32[2048]{0:T(1024)S(1)} fusion(f32[2048,1024]{0,1:T(8,128)S(1)} %get-tuple-element.31, f32[2048]{0:T(1024)S(1)} %broadcast_maximum_fusion, s32[2048]{0:T(1024)S(1)} %bitcast.51, s32[2048]{0:T(1024)S(1)} %bitcast.48, s32[1024]{0:T(1024)S(1)} %get-tuple-element.7, s32[1024]{0:T(1024)S(1)} %convert_reduce_fusion), kind=kLoop, calls=%fused_computation.10 | loop fusion | flops 16775168 | bytes 8429568 | tf_op jit(solution)/shard_map/reduce_sum | solution.py:92
  317.9 3.1 fusion.14
  320.9 0.9 copy.34
  (29 shorter events, 0.5 us)
Async XLA Ops:
  6.5 6.6 %copy-start = (s32[1024]{0:T(1024)S(1)}, s32[1024]{0:T(1024)}, u32[]{:S(2)}) copy-start(s32[1024]{0:T(1024)} %param.7) | copy-start | bytes 12292
  6.5 227.1 %all-reduce.3.cloned.1.call-start = ((), (), s32[]{:S(2)}) async-start(), calls=%async_computation.2 | async-start | bytes 8388608 | tf_op jit(solution)/shard_map/psum | solution.py:54
  74.6 187.6 %reduce-scatter.5.cloned.1.call-start = ((), (), s32[]{:S(2)}) async-start(), calls=%async_computation.4 | async-start | bytes 1310720 | tf_op jit(solution)/shard_map/reduce_scatter | solution.py:62
  238.1 10.0 %copy-start.2 = (s32[8]{0:T(128)S(1)}, s32[8]{0:T(128)}, u32[]{:S(2)}) copy-start(s32[8]{0:T(128)} %param.8) | copy-start | bytes 100
  238.1 10.4 %copy-start.3 = (u32[32]{0:T(128)S(1)}, u32[32]{0:T(128)}, u32[]{:S(2)}) copy-start(u32[32]{0:T(128)} %constant.126) | copy-start | bytes 388
  238.1 71.2 %reduce-scatter.3.cloned.1.call-start = ((), (), s32[]{:S(2)}) async-start(), calls=%async_computation.3 | async-start | bytes 5242880 | tf_op jit(solution)/shard_map/reduce_scatter | solution.py:61
  314.1 7.8 %copy-start.1 = (s32[1024]{0:T(1024)S(1)}, s32[1024]{0:T(1024)}, u32[]{:S(2)}) copy-start(s32[1024]{0:T(1024)} %param.7) | copy-start | bytes 12292
Sparse Core Ops, SparseCore 0:
  74.7 158.8 all-reduce.2
  238.2 23.8 reduce-scatter.4
  264.7 44.5 reduce-scatter.2
where the time goes:
time: 330 us; the launch traced here: 328 us
  waiting for transfers between devices  192 us (58%)
  local copies, waits for them, and re-layouts  63.5 us (19%)
  other arithmetic  20.2 us (6%)
  matrix products  19.5 us (6%)
  blocking collectives  19.1 us (6%)
  between operations  14 us (4%)
    psum x1, waiting for transfers between devices, shards(): col_embed = lax.psum(partial_value, 'tp').astype(jnp.float32)  156 us
    gather x1, local copies, waits for them, and re-layouts, shards(): picked = jnp.take(table, jnp.clip(local_ids, 0, vocab_here - 1), axis=0)  52.7 us
    reduce_scatter x1, waiting for transfers between devices, shards(): lax.psum_scatter(query_term, 'ctx', scatter_dimension=0, tiled=True)  33.6 us
    dot_general x1, matrix products, shards(): jnp.dot(col_scaled, w_query, preferred_element_type=jnp.float32)  9.92 us
    unnamed x1, blocking collectives  7.27 us
  transfers between devices with their start and end apart: 3, of which 3 were waited for; matrix products, arithmetic and copies ran while one was open for 6% of the time, Pallas kernels for 0%

commit v1 on v0

--- a/solution.py
+++ b/solution.py
@@ -8,6 +8,11 @@
 HD = 128
 BLOCK = 128
 rotary_base = 500000.0
+
+
+def gather_and_add(x, axis):
+    pieces = lax.all_gather(x, axis)
+    return jnp.sum(pieces, axis=0)
 
 
 def rotary(values_in, pos_rows):
@@ -51,7 +56,7 @@
     w_pair = lax.dynamic_slice_in_dim(w_keyval, kv_head * HD, HD, 2).reshape(
         w_keyval.shape[0], 2 * HD
     )
-    col_embed = lax.psum(partial_value, "tp").astype(jnp.float32)
+    col_embed = gather_and_add(partial_value, "tp").astype(jnp.float32)
     gain_here = lax.dynamic_slice_in_dim(gain, ctx_at * columns, columns)
     col_scaled = (col_embed * gain_here).astype(jnp.bfloat16)
     query_term = jnp.dot(col_scaled, w_query, preferred_element_type=jnp.float32)

time: 330 us -> 826 us (2.50)
  waiting for transfers between devices: 192 us -> 674 us
  other arithmetic: 20.2 us -> 34.6 us
    all_gather x0 -> x1, waiting for transfers between devices: none -> 638 us  [gather_and_add(): pieces = lax.all_gather(x, axis)]
    psum x1 -> x0, waiting for transfers between devices: 156 us -> none  [shards(): col_embed = lax.psum(partial_value, 'tp').astype(jnp.float32)]
    reduce_sum x0 -> x1, other arithmetic: none -> 14.2 us  [gather_and_add(): return jnp.sum(pieces, axis=0)]
  transfers between devices with their start and end apart: 3 -> 3, of which waited for: 3 -> 3; matrix products, arithmetic and copies ran while one was open for 6% -> 2% of each run, Pallas kernels for 0% -> 0%
where the time goes in v1:
time: 826 us; the launch traced here: 825 us
  waiting for transfers between devices  674 us (82%)
  local copies, waits for them, and re-layouts  63.4 us (8%)
  other arithmetic  34.6 us (4%)
  matrix products  19.6 us (2%)
  blocking collectives  19.1 us (2%)
  between operations  14 us (2%)
    all_gather x1, waiting for transfers between devices, gather_and_add(): pieces = lax.all_gather(x, axis)  638 us
    gather x1, local copies, waits for them, and re-layouts, shards(): picked = jnp.take(table, jnp.clip(local_ids, 0, vocab_here - 1), axis=0)  52.7 us
    reduce_scatter x1, waiting for transfers between devices, shards(): lax.psum_scatter(query_term, 'ctx', scatter_dimension=0, tiled=True)  33.6 us
  transfers between devices with their start and end apart: 3, of which 3 were waited for; matrix products, arithmetic and copies ran while one was open for 2% of the time, Pallas kernels for 0%

profile of v1, /device:TPU:0, one launch (start us, length us, event | category | flops | bytes accessed | tf_op | source)
XLA Modules:
  0.0 825.0 jit_solution(1896347978864197796)
XLA Ops:
  6.6 1.6 fusion.33
  8.2 4.3 compare_select_fusion.3
  12.5 0.7 fusion.22
  13.2 4.5 gather_fusion
  17.8 52.7 %gather_fusion.1 = bf16[1024,2048]{1,0:T(8,128)(2,1)} fusion(bf16[16032,2048]{1,0:T(8,128)(2,1)} %param.10, s32[1024]{0:T(1024)S(1)} %broadcast_clamp_fusion), kind=kCustom, calls=%fused_computation.1 | custom fusion | bytes 8392704 | tf_op jit(solution)/shard_map/jit(_take)/gather | solution.py:53
  70.5 4.1 fusion.5
  74.7 0.7 dynamic_slice.10
  75.4 1.8 constant_dynamic-slice_fusion
  77.2 637.7 %all-gather.2.cloned.1.call-done = bf16[8,1024,2048]{2,1,0:T(8,128)(2,1)} async-done(((bf16[1,1024,2048]{2,1,0:T(8,128)(2,1)}), bf16[8,1024,2048]{2,1,0:T(8,128)(2,1)}) %all-gather.2.cloned.1.call-update) | async-done | bytes 33554448 | tf_op jit(solution)/shard_map/all_gather | solution.py:14
  715.0 14.2 %reduce_sum.50 = bf16[1024,2048]{1,0:T(8,128)(2,1)} reduce(bf16[8,1024,2048]{2,1,0:T(8,128)(2,1)} %all-gather.2.cloned.1.call-done, bf16[]{:T(256)} %constant.105.clone.1), dimensions={0}, to_apply=%region_3.4 | reduce | flops 14680064 | bytes 37748736 | tf_op jit(solution)/shard_map/reduce_sum | solution.py:15
  729.2 4.5 fusion.8
  733.8 9.9 %fusion.10 = f32[1024,1024]{1,0:T(8,128)} fusion(bf16[2048,1024]{1,0:T(8,128)(2,1)} %param.12, bf16[1024,2048]{1,0:T(8,128)(2,1)} %reduce_sum.50, f32[2048]{0:T(1024)S(1)} %dynamic_slice.10), kind=kOutput, calls=%fused_computation.16 | convolution fusion | flops 4301258752 | bytes 12591104 | tf_op jit(solution)/shard_map/dot_general | solution.py:62
  743.7 0.2 reduce-window.8
  744.1 0.6 dynamic-slice
  745.4 3.1 fusion.1
  748.5 7.3 all-reduce
  755.9 2.9 reduce-scatter.5.cloned.1.call-done
  758.8 1.1 slice_multiply_fusion.1
  759.8 0.6 subtract_convert_fusion.1
  760.4 0.1 pad_maximum_fusion.1
  760.5 5.8 all_gather.11
  766.3 6.0 all_gather.12
  772.3 33.6 %reduce-scatter.3.cloned.1.call-done = f32[256,1024]{1,0:T(8,128)} async-done(((f32[1024,1024]{1,0:T(8,128)}), f32[256,1024]{1,0:T(8,128)}) %reduce-scatter.3.cloned.1.call-update) | async-done | bytes 1048592 | tf_op jit(solution)/shard_map/reduce_scatter | solution.py:66
  805.9 1.4 multiply_bitcast_fusion
  807.2 0.2 copy.23
  807.4 0.3 fusion.32
  807.8 0.4 subtract_convert_fusion
  808.2 0.3 pad_maximum_fusion
  808.5 2.1 fusion.2
  810.7 3.8 fusion.3
  814.4 3.1 fusion.15
  817.5 0.9 copy.34
  (30 shorter events, 0.6 us)
Async XLA Ops:
  6.5 6.6 copy-start
  6.5 708.4 %all-gather.2.cloned.1.call-start = ((), (), s32[]{:S(2)}) async-start(), calls=%async_computation.2 | async-start | bytes 37748736 | tf_op jit(solution)/shard_map/all_gather | solution.py:14
  74.6 684.1 %reduce-scatter.5.cloned.1.call-start = ((), (), s32[]{:S(2)}) async-start(), calls=%async_computation.4 | async-start | bytes 1310720 | tf_op jit(solution)/shard_map/reduce_scatter | solution.py:67
  733.7 10.0 %copy-start.2 = (s32[8]{0:T(128)S(1)}, s32[8]{0:T(128)}, u32[]{:S(2)}) copy-start(s32[8]{0:T(128)} %param.8) | copy-start | bytes 100
  733.7 10.4 %copy-start.3 = (u32[32]{0:T(128)S(1)}, u32[32]{0:T(128)}, u32[]{:S(2)}) copy-start(u32[32]{0:T(128)} %constant.127) | copy-start | bytes 388
  733.7 72.1 %reduce-scatter.3.cloned.1.call-start = ((), (), s32[]{:S(2)}) async-start(), calls=%async_computation.3 | async-start | bytes 5242880 | tf_op jit(solution)/shard_map/reduce_scatter | solution.py:66
  810.6 7.8 copy-start.1
Sparse Core Ops, SparseCore 0:
  74.8 640.1 all-gather.1
  733.8 24.8 reduce-scatter.4
  761.3 44.5 reduce-scatter.2
